TPU v7x, 32 devices: a whole 2x2x4 slice. The times are simulated.
32 devices in a mesh: group: 1, expert: 16 (over z, y, x), step: 2 (over core).
Axes of the slice: x: 2, y: 2, z: 4, core: 2. Of those that a mesh axis runs over, the one named last changes fastest.
Arguments:
- latents: float32 [2, 2048, 1536], P('step', ('group', 'expert')), may hold values from -6 to 6
- modulation: float32 [2, 6, 1536], P('group'), may hold values from -3 to 3
- shallow_routes: int32 [2, 2048, 2], P('step', ('group', 'expert')), may hold values from 0 to 3, all different within a row; in each aligned block of 128 rows (0 to 127, 128 to 255, ..., all dimensions but the last counted through in order) at most 64 rows name the same one
- deep_routes: int32 [2048, 2], P(('group', 'expert')), may hold values from 0 to 3, all different within a row; in each aligned block of 128 rows (0 to 127, 128 to 255, ...) at most 64 rows name the same one
- refresh: int32 [16], P(('group', 'expert')), may hold values from 0 to 1
- shallow_in: bfloat16 [16, 1536, 768], P('expert'), may hold values from -0.15625 to 0.15625
- shallow_out: bfloat16 [16, 768, 1536], P('expert'), may hold values from -0.109375 to 0.109375
- deep_in: bfloat16 [16, 1536, 768], P('expert'), may hold values from -0.15625 to 0.15625
- deep_out: bfloat16 [16, 768, 1536], P('expert'), may hold values from -0.109375 to 0.109375
- shallow_router: float32 [1536, 4], replicated, may hold values from -0.15625 to 0.15625
- deep_router: float32 [1536, 4], replicated, may hold values from -0.15625 to 0.15625
Outputs:
- result: bfloat16 [2, 2048, 1536], P('step', ('group', 'expert'))
Inputs may be any that keep to these rules, and one draw needn't show every extreme that they name: `shallow_routes`: within the 128 rows of one index of expert (aligned blocks), each expert is named by at most 64 rows, and by exactly 64 rows in some block; a row names two different experts. `deep_routes`: within the 128 rows of one index of expert (aligned blocks), each expert is named by at most 64 rows, and by exactly 64 rows in some block; a row names two different experts.
All inputs are finite; a program needn't handle non-finite values.
Results may differ from a plain program's by a relative error of at most 0.01.
Values may be sent and summed in bfloat16 or wider, within the bound.
No kernel may reach another device: no remote copies, remote signals or barrier semaphores. Data moves between devices by JAX's collectives and lax.ppermute only.
A program may use at most 64 MiB of HBM per device.

v0:
```python
import jax
import jax.numpy as jnp
from jax import lax
from jax.sharding import PartitionSpec as P


def from_root(block, axis, owner):
    block = jnp.where(lax.axis_index(axis) == owner, block, jnp.zeros_like(block))
    return lax.psum(block, axis)


def modulate(hidden, shift_row, scale_row):
    average = jnp.mean(hidden, axis=-1, keepdims=True)
    centred = hidden - average
    variance = jnp.mean(centred * centred, axis=-1, keepdims=True)
    return (centred * lax.rsqrt(variance + 1e-06) * (1.0 + scale_row) + shift_row).astype(
        jnp.bfloat16
    )


def plan(normed, routes, router, capacity):
    rows_count, width = normed.shape
    experts = router.shape[1]
    logits = jnp.dot(normed.astype(jnp.float32), router, precision=lax.Precision.HIGHEST)
    hits = routes[:, :, None] == jnp.arange(experts, dtype=jnp.int32)
    chosen = jnp.sum(jnp.where(hits, logits[:, None, :], 0.0), axis=-1)
    gate_sig = jax.nn.sigmoid(chosen)
    weights = gate_sig / jnp.sum(gate_sig, axis=-1, keepdims=True)
    pair_hits = hits.reshape(rows_count * 2, experts).astype(jnp.int32)
    position = jnp.sum(pair_hits * (jnp.cumsum(pair_hits, axis=0) - 1), axis=-1).reshape(
        rows_count, 2
    )
    slot_hit = position[:, :, None] == jnp.arange(capacity, dtype=jnp.int32)
    placed = hits[:, :, :, None] & slot_hit[:, :, None, :]
    dispatch = jnp.any(placed, axis=1).reshape(rows_count, experts * capacity).astype(jnp.bfloat16)
    gathered = jnp.einsum("rs,rd->sd", dispatch, normed, preferred_element_type=jnp.float32).astype(
        jnp.bfloat16
    )
    combine_w = jnp.sum(jnp.where(placed, weights[:, :, None, None], 0.0), axis=1)
    return (gathered.reshape(experts, capacity, width), combine_w)


def spread(gathered, slices):
    experts, capacity, width = gathered.shape
    quarters = slices // experts
    return jnp.broadcast_to(gathered[:, None], (experts, quarters, capacity, width)).reshape(
        slices, capacity, width
    )


def expert_rows(piece, weight_in, weight_out):
    dims = piece.shape
    flat_rows = piece.reshape(-1, dims[-1])
    hidden = jax.nn.gelu(
        jnp.dot(flat_rows, weight_in, preferred_element_type=jnp.float32), approximate=True
    ).astype(jnp.bfloat16)
    return (
        jnp.dot(hidden, weight_out, preferred_element_type=jnp.float32)
        .astype(jnp.bfloat16)
        .reshape(dims)
    )


def combine(summed, combine_w):
    rows_count = combine_w.shape[0]
    width = summed.shape[-1]
    return jnp.dot(
        combine_w.reshape(rows_count, -1),
        summed.reshape(-1, width),
        precision=lax.Precision.HIGHEST,
        preferred_element_type=jnp.float32,
    )


def finish(returned, combine_w):
    experts = combine_w.shape[1]
    width = returned.shape[2]
    summed = jnp.sum(
        returned.astype(jnp.float32).reshape(experts, -1, returned.shape[1], width), axis=1
    )
    return combine(summed, combine_w)


def body(
    latents,
    modulation,
    shallow_routes,
    deep_routes,
    refresh,
    shallow_in,
    shallow_out,
    deep_in,
    deep_out,
    shallow_router,
    deep_router,
):
    slices = lax.axis_size("expert")
    experts = shallow_router.shape[1]
    rows_count = latents.shape[1]
    capacity = 2 * max(rows_count * 5 // 64, rows_count // experts)
    step_idx = lax.axis_index("step")
    root_idx = refresh[0]
    own_mod = lax.dynamic_index_in_dim(modulation, step_idx, 0, keepdims=False)
    features = latents[0]
    normed = modulate(features, own_mod[0], own_mod[1])
    gathered, combine_w = plan(normed, shallow_routes[0], shallow_router, capacity)
    partial_value = expert_rows(
        lax.all_to_all(spread(gathered, slices), "expert", split_axis=0, concat_axis=0, tiled=True),
        shallow_in[0],
        shallow_out[0],
    )
    returned = lax.all_to_all(partial_value, "expert", split_axis=0, concat_axis=0, tiled=True)
    moe_shallow = finish(returned, combine_w)
    after_shallow = (features + own_mod[2] * moe_shallow).astype(jnp.bfloat16)
    normed_deep = modulate(after_shallow.astype(jnp.float32), own_mod[3], own_mod[4])
    gathered_deep, combine_deep = plan(normed_deep, deep_routes, deep_router, capacity)
    partial_value = expert_rows(
        lax.all_to_all(
            spread(gathered_deep, slices), "expert", split_axis=0, concat_axis=0, tiled=True
        ),
        deep_in[0],
        deep_out[0],
    )
    returned_deep = lax.all_to_all(partial_value, "expert", split_axis=0, concat_axis=0, tiled=True)
    moe_deep = finish(returned_deep, combine_deep)
    own_delta = (own_mod[5] * moe_deep).astype(jnp.bfloat16)
    deep_delta = from_root(own_delta, "step", root_idx)
    result = (after_shallow.astype(jnp.float32) + deep_delta.astype(jnp.float32)).astype(
        jnp.bfloat16
    )
    return result[None]


def solution(mesh):
    in_specs = (
        P("step", ("group", "expert"), None),
        P("group", None, None),
        P("step", ("group", "expert"), None),
        P(("group", "expert"), None),
        P(("group", "expert")),
        P("expert", None, None),
        P("expert", None, None),
        P("expert", None, None),
        P("expert", None, None),
        P(),
        P(),
    )
    out_specs = P("step", ("group", "expert"), None)
    return jax.shard_map(body, mesh=mesh, in_specs=in_specs, out_specs=out_specs, check_vma=False)
```

profile of v0, /device:TPU:0, one launch (start us, length us, event | category | flops | bytes accessed | tf_op | source)
XLA Modules:
  0.0 376.2 jit_solution(6678324923360058093)
XLA Ops:
  6.5 0.9 copy.32
  7.8 1.3 reduce_sum.127
  9.0 1.4 multiply_reduce_fusion.1
  10.4 0.7 iota_compare_fusion.5
  11.1 1.2 reduce-window.14
  13.0 0.9 dynamic-slice_reduce_fusion.1
  13.9 1.6 convolution_convert_fusion.3
  15.9 79.5 %all_to_all.20 = bf16[16,64,1536]{2,1,0:T(8,128)(2,1)} all-to-all(bf16[16,64,1536]{2,1,0:T(8,128)(2,1)S(1)} %bitcast.112), channel_id=1, replica_groups=mesh['group'=1,'expert'=16,'step'=2] {'expert'}, dimensions={0} | all-to-all | bytes 6291456 | tf_op jit(solution)/shard_map/all_to_all | solution.py:108
  95.4 10.4 %convolution_convert_fusion.1 = bf16[1024,1536]{1,0:T(8,128)(2,1)} fusion(bf16[1,768,1536]{2,1,0:T(8,128)(2,1)S(1)} %copy-done, bf16[1024,1536]{1,0:T(8,128)(2,1)} %bitcast.116, bf16[1,1536,768]{2,1,0:T(8,128)(2,1)} %param.16), kind=kOutput, calls=%fused_computation.5 | convolution fusion | flops 4840488960 | bytes 11010048 | tf_op jit(solution)/shard_map/dot_general | solution.py:58
  105.8 4.6 %all-to-all-start.1 = ((bf16[16,64,1536]{2,1,0:T(8,128)(2,1)}), bf16[16,64,1536]{2,1,0:T(8,128)(2,1)}, u32[]{:S(2)}, u32[]{:S(2)}) async-start(bf16[16,64,1536]{2,1,0:T(8,128)(2,1)} %bitcast.114), calls=%async_computation.1 | async-start | bytes 6291456 | tf_op jit(solution)/shard_map/all_to_all | solution.py:112
  110.9 1.2 reduce-window.16
  112.7 0.5 fusion.44
  113.5 57.2 %all-to-all-done.1 = bf16[16,64,1536]{2,1,0:T(8,128)(2,1)} async-done(((bf16[16,64,1536]{2,1,0:T(8,128)(2,1)}), bf16[16,64,1536]{2,1,0:T(8,128)(2,1)}, u32[]{:S(2)}, u32[]{:S(2)}) %all-to-all-start.1) | async-done | bytes 3145760 | tf_op jit(solution)/shard_map/all_to_all | solution.py:112
  170.7 2.6 convert_reduce_fusion.1
  173.2 1.1 fusion.61
  175.5 84.7 %all_to_all.21 = bf16[16,64,1536]{2,1,0:T(8,128)(2,1)} all-to-all(bf16[16,64,1536]{2,1,0:T(8,128)(2,1)S(1)} %bitcast.113), channel_id=1, replica_groups=mesh['group'=1,'expert'=16,'step'=2] {'expert'}, dimensions={0} | all-to-all | bytes 6291456 | tf_op jit(solution)/shard_map/all_to_all | solution.py:118
  260.3 11.1 %convolution_convert_fusion = bf16[1024,1536]{1,0:T(8,128)(2,1)} fusion(bf16[1,768,1536]{2,1,0:T(8,128)(2,1)} %param.19, bf16[1024,1536]{1,0:T(8,128)(2,1)} %bitcast.117, bf16[1,1536,768]{2,1,0:T(8,128)(2,1)} %param.18), kind=kOutput, calls=%fused_computation.4 | convolution fusion | flops 4840488960 | bytes 11010048 | tf_op jit(solution)/shard_map/dot_general | solution.py:58
  271.4 4.6 %all-to-all-start.3 = ((bf16[16,64,1536]{2,1,0:T(8,128)(2,1)}), bf16[16,64,1536]{2,1,0:T(8,128)(2,1)}, u32[]{:S(2)}, u32[]{:S(2)}) async-start(bf16[16,64,1536]{2,1,0:T(8,128)(2,1)} %bitcast.115), calls=%async_computation.3 | async-start | bytes 6291456 | tf_op jit(solution)/shard_map/all_to_all | solution.py:124
  276.7 0.4 fusion.62
  277.3 58.9 %all-to-all-done.3 = bf16[16,64,1536]{2,1,0:T(8,128)(2,1)} async-done(((bf16[16,64,1536]{2,1,0:T(8,128)(2,1)}), bf16[16,64,1536]{2,1,0:T(8,128)(2,1)}, u32[]{:S(2)}, u32[]{:S(2)}) %all-to-all-start.3) | async-done | bytes 3145760 | tf_op jit(solution)/shard_map/all_to_all | solution.py:124
  336.2 2.6 convert_reduce_fusion
  338.7 1.7 fusion.22
  340.5 27.0 %all-reduce.2.cloned.1.call-done = bf16[128,1536]{1,0:T(8,128)(2,1)} async-done(((bf16[128,1536]{1,0:T(8,128)(2,1)}), bf16[128,1536]{1,0:T(8,128)(2,1)}) %all-reduce.2.cloned.1.call-update) | async-done | bytes 393232 | tf_op jit(solution)/shard_map/psum | solution.py:9
  367.6 1.8 fusion.39
  (65 shorter events, 3.8 us)
Async XLA Ops:
  6.5 88.8 %copy-start = (bf16[1,768,1536]{2,1,0:T(8,128)(2,1)S(1)}, bf16[1,768,1536]{2,1,0:T(8,128)(2,1)}, u32[]{:S(2)}) copy-start(bf16[1,768,1536]{2,1,0:T(8,128)(2,1)} %param.17) | copy-start | bytes 7077892
  105.8 4.7 %copy-start.7 = (s32[128,2]{0,1:T(2,128)S(1)}, s32[128,2]{0,1:T(2,128)}, u32[]{:S(2)}) copy-start(s32[128,2]{0,1:T(2,128)} %param.14) | copy-start | bytes 3076
  105.8 6.9 %copy-start.1 = (f32[1,128,1536]{2,1,0:T(8,128)S(1)}, f32[1,128,1536]{2,1,0:T(8,128)}, u32[]{:S(2)}) copy-start(f32[1,128,1536]{2,1,0:T(8,128)} %param.11) | copy-start | bytes 2359300
  105.8 6.9 %copy-start.4 = (f32[1536,4]{0,1:T(4,128)S(1)}, f32[1536,4]{0,1:T(4,128)}, u32[]{:S(2)}) copy-start(f32[1536,4]{0,1:T(4,128)} %param.20) | copy-start | bytes 73732
  105.8 7.4 %copy-start.6 = (s32[1,128,2]{1,2,0:T(2,128)S(1)}, s32[1,128,2]{1,2,0:T(2,128)}, u32[]{:S(2)}) copy-start(s32[1,128,2]{1,2,0:T(2,128)} %param.13) | copy-start | bytes 3076
  105.8 64.8 %all-to-all-start.1 = ((bf16[16,64,1536]{2,1,0:T(8,128)(2,1)}), bf16[16,64,1536]{2,1,0:T(8,128)(2,1)}, u32[]{:S(2)}, u32[]{:S(2)}) async-start(bf16[16,64,1536]{2,1,0:T(8,128)(2,1)} %bitcast.114), calls=%async_computation.1 | async-start | bytes 6291456 | tf_op jit(solution)/shard_map/all_to_all | solution.py:112
  174.3 0.9 copy-start.2
  271.4 5.3 %copy-start.5 = (f32[1536,4]{0,1:T(4,128)S(1)}, f32[1536,4]{0,1:T(4,128)}, u32[]{:S(2)}) copy-start(f32[1536,4]{0,1:T(4,128)} %param.21) | copy-start | bytes 73732
  271.4 64.8 %all-to-all-start.3 = ((bf16[16,64,1536]{2,1,0:T(8,128)(2,1)}), bf16[16,64,1536]{2,1,0:T(8,128)(2,1)}, u32[]{:S(2)}, u32[]{:S(2)}) async-start(bf16[16,64,1536]{2,1,0:T(8,128)(2,1)} %bitcast.115), calls=%async_computation.3 | async-start | bytes 6291456 | tf_op jit(solution)/shard_map/all_to_all | solution.py:124
  276.0 91.6 %all-reduce.2.cloned.1.call-start = ((), (), s32[]{:S(2)}) async-start(), calls=%async_computation.4 | async-start | bytes 786432 | tf_op jit(solution)/shard_map/psum | solution.py:9
  277.3 90.3 %copy-start.3 = (f32[128,1536]{1,0:T(8,128)S(1)}, f32[128,1536]{1,0:T(8,128)}, u32[]{:S(2)}) copy-start(f32[128,1536]{1,0:T(8,128)} %copy-done.2) | copy-start | bytes 2359300
Sparse Core Ops, SparseCore 0:
  340.6 26.8 all-reduce.1
where the time goes:
time: 377 us; the launch traced here: 376 us
  blocking collectives  164 us (44%)
  waiting for transfers between devices  143 us (38%)
  matrix products  27.3 us (7%)
  other arithmetic  14.7 us (4%)
  between operations  14.3 us (4%)
  starting transfers between devices  9.3 us (2%)
    all_to_all x2, waiting for transfers between devices, body(): lax.all_to_all(partial_value, 'expert', split_axis=0, concat_axis=0, tile...  116 us
    all_to_all x1, blocking collectives, body(): lax.all_to_all(spread(gathered_deep, slices), 'expert', split_axis=0, con...  84.7 us
    all_to_all x1, blocking collectives, body(): lax.all_to_all(spread(gathered, slices), 'expert', split_axis=0, concat_a...  79.5 us
    psum x1, waiting for transfers between devices, from_root(): return lax.psum(block, axis)  27 us
    dot_general x2, matrix products, expert_rows(): jnp.dot(hidden, weight_out, preferred_element_type=jnp.float32)  21.5 us
    all_to_all x2, starting transfers between devices, body(): lax.all_to_all(partial_value, 'expert', split_axis=0, concat_axis=0, tile...  9.25 us
  transfers between devices with their start and end apart: 3, of which 3 were waited for; matrix products, arithmetic and copies ran while one was open for 1% of the time, Pallas kernels for 0%

commit v1 on v0

--- a/solution.py
+++ b/solution.py
@@ -6,7 +6,7 @@
 
 def from_root(block, axis, owner):
     block = jnp.where(lax.axis_index(axis) == owner, block, jnp.zeros_like(block))
-    return lax.psum(block, axis)
+    return jnp.sum(lax.all_gather(block, axis), axis=0)
 
 
 def modulate(hidden, shift_row, scale_row):

time: 377 us -> 347 us (0.920)
  the two profiles are of different devices: /device:TPU:0 before, /device:TPU:13 now
where the time goes in v1:
time: 347 us; the launch traced here: 346 us
  blocking collectives  154 us (44%)
  waiting for transfers between devices  137 us (39%)
  matrix products  26.5 us (8%)
  other arithmetic  15 us (4%)
  starting transfers between devices  10.1 us (3%)
    all_to_all x2, waiting for transfers between devices, body(): lax.all_to_all(partial_value, 'expert', split_axis=0, concat_axis=0, tile...  137 us
    all_to_all x1, blocking collectives, body(): lax.all_to_all(spread(gathered, slices), 'expert', split_axis=0, concat_a...  76.2 us
    all_to_all x1, blocking collectives, body(): lax.all_to_all(spread(gathered_deep, slices), 'expert', split_axis=0, con...  73.9 us
    dot_general x2, matrix products, expert_rows(): jnp.dot(hidden, weight_out, preferred_element_type=jnp.float32)  21.5 us
    all_to_all x2, starting transfers between devices, body(): lax.all_to_all(partial_value, 'expert', split_axis=0, concat_axis=0, tile...  10.1 us
  transfers between devices with their start and end apart: 2, of which 2 were waited for; matrix products, arithmetic and copies ran while one was open for 1% of the time, Pallas kernels for 0%

profile of v1, /device:TPU:13, one launch (start us, length us, event | category | flops | bytes accessed | tf_op | source)
XLA Modules:
  0.0 346.2 jit_solution(7170594384440726311)
XLA Ops:
  0.0 0.9 copy.32
  1.2 1.3 reduce_sum.139
  2.5 1.4 multiply_reduce_fusion.1
  3.9 0.7 iota_compare_fusion.5
  4.6 1.2 reduce-window.14
  6.5 0.9 dynamic-slice_reduce_fusion.1
  7.4 1.6 convolution_convert_fusion.3
  9.3 76.2 %all_to_all.20 = bf16[16,64,1536]{2,1,0:T(8,128)(2,1)} all-to-all(bf16[16,64,1536]{2,1,0:T(8,128)(2,1)S(1)} %bitcast.113), channel_id=1, replica_groups=mesh['group'=1,'expert'=16,'step'=2] {'expert'}, dimensions={0} | all-to-all | bytes 6291456 | tf_op jit(solution)/shard_map/all_to_all | solution.py:108
  85.5 10.4 %convolution_convert_fusion.1 = bf16[1024,1536]{1,0:T(8,128)(2,1)} fusion(bf16[1,768,1536]{2,1,0:T(8,128)(2,1)S(1)} %copy-done, bf16[1024,1536]{1,0:T(8,128)(2,1)} %bitcast.117, bf16[1,1536,768]{2,1,0:T(8,128)(2,1)} %param.16), kind=kOutput, calls=%fused_computation.5 | convolution fusion | flops 4840488960 | bytes 11010048 | tf_op jit(solution)/shard_map/dot_general | solution.py:58
  95.9 5.0 %all-to-all-start.1 = ((bf16[16,64,1536]{2,1,0:T(8,128)(2,1)}), bf16[16,64,1536]{2,1,0:T(8,128)(2,1)}, u32[]{:S(2)}, u32[]{:S(2)}) async-start(bf16[16,64,1536]{2,1,0:T(8,128)(2,1)} %bitcast.115), calls=%async_computation.1 | async-start | bytes 6291456 | tf_op jit(solution)/shard_map/all_to_all | solution.py:112
  101.3 1.2 reduce-window.16
  103.2 0.5 fusion.44
  103.9 67.6 %all-to-all-done.1 = bf16[16,64,1536]{2,1,0:T(8,128)(2,1)} async-done(((bf16[16,64,1536]{2,1,0:T(8,128)(2,1)}), bf16[16,64,1536]{2,1,0:T(8,128)(2,1)}, u32[]{:S(2)}, u32[]{:S(2)}) %all-to-all-start.1) | async-done | bytes 3145760 | tf_op jit(solution)/shard_map/all_to_all | solution.py:112
  171.5 2.6 convert_reduce_fusion.1
  174.1 1.1 fusion.61
  176.4 73.9 %all_to_all.21 = bf16[16,64,1536]{2,1,0:T(8,128)(2,1)} all-to-all(bf16[16,64,1536]{2,1,0:T(8,128)(2,1)S(1)} %bitcast.114), channel_id=1, replica_groups=mesh['group'=1,'expert'=16,'step'=2] {'expert'}, dimensions={0} | all-to-all | bytes 6291456 | tf_op jit(solution)/shard_map/all_to_all | solution.py:118
  250.2 11.1 %convolution_convert_fusion = bf16[1024,1536]{1,0:T(8,128)(2,1)} fusion(bf16[1,768,1536]{2,1,0:T(8,128)(2,1)} %param.19, bf16[1024,1536]{1,0:T(8,128)(2,1)} %bitcast.118, bf16[1,1536,768]{2,1,0:T(8,128)(2,1)} %param.18), kind=kOutput, calls=%fused_computation.4 | convolution fusion | flops 4840488960 | bytes 11010048 | tf_op jit(solution)/shard_map/dot_general | solution.py:58
  261.4 5.1 %all-to-all-start.3 = ((bf16[16,64,1536]{2,1,0:T(8,128)(2,1)}), bf16[16,64,1536]{2,1,0:T(8,128)(2,1)}, u32[]{:S(2)}, u32[]{:S(2)}) async-start(bf16[16,64,1536]{2,1,0:T(8,128)(2,1)} %bitcast.116), calls=%async_computation.3 | async-start | bytes 6291456 | tf_op jit(solution)/shard_map/all_to_all | solution.py:124
  267.6 69.4 %all-to-all-done.3 = bf16[16,64,1536]{2,1,0:T(8,128)(2,1)} async-done(((bf16[16,64,1536]{2,1,0:T(8,128)(2,1)}), bf16[16,64,1536]{2,1,0:T(8,128)(2,1)}, u32[]{:S(2)}, u32[]{:S(2)}) %all-to-all-start.3) | async-done | bytes 3145760 | tf_op jit(solution)/shard_map/all_to_all | solution.py:124
  337.0 2.6 convert_reduce_fusion
  339.6 1.0 fusion.22
  340.6 3.5 %all-gather = bf16[256,1536]{1,0:T(8,128)(2,1)} all-gather(bf16[128,1536]{1,0:T(8,128)(2,1)S(1)} %fusion.22), channel_id=2, replica_groups=mesh['group'=1,'expert'=16,'step'=2] {'step'}, dimensions={0}, use_global_device_ids=true | all-gather | bytes 1179648 | tf_op jit(solution)/shard_map/all_gather | solution.py:9
  344.1 1.3 reduce_sum.152
  345.4 0.8 fusion.39
  (64 shorter events, 4.2 us)
Async XLA Ops:
  0.0 85.5 %copy-start = (bf16[1,768,1536]{2,1,0:T(8,128)(2,1)S(1)}, bf16[1,768,1536]{2,1,0:T(8,128)(2,1)}, u32[]{:S(2)}) copy-start(bf16[1,768,1536]{2,1,0:T(8,128)(2,1)} %param.17) | copy-start | bytes 7077892
  95.9 5.0 %copy-start.7 = (s32[128,2]{0,1:T(2,128)S(1)}, s32[128,2]{0,1:T(2,128)}, u32[]{:S(2)}) copy-start(s32[128,2]{0,1:T(2,128)} %param.14) | copy-start | bytes 3076
  95.9 7.3 %copy-start.1 = (f32[1,128,1536]{2,1,0:T(8,128)S(1)}, f32[1,128,1536]{2,1,0:T(8,128)}, u32[]{:S(2)}) copy-start(f32[1,128,1536]{2,1,0:T(8,128)} %param.11) | copy-start | bytes 2359300
  95.9 7.3 %copy-start.4 = (f32[1536,4]{0,1:T(4,128)S(1)}, f32[1536,4]{0,1:T(4,128)}, u32[]{:S(2)}) copy-start(f32[1536,4]{0,1:T(4,128)} %param.20) | copy-start | bytes 73732
  95.9 7.8 %copy-start.6 = (s32[1,128,2]{1,2,0:T(2,128)S(1)}, s32[1,128,2]{1,2,0:T(2,128)}, u32[]{:S(2)}) copy-start(s32[1,128,2]{1,2,0:T(2,128)} %param.13) | copy-start | bytes 3076
  95.9 75.6 %all-to-all-start.1 = ((bf16[16,64,1536]{2,1,0:T(8,128)(2,1)}), bf16[16,64,1536]{2,1,0:T(8,128)(2,1)}, u32[]{:S(2)}, u32[]{:S(2)}) async-start(bf16[16,64,1536]{2,1,0:T(8,128)(2,1)} %bitcast.115), calls=%async_computation.1 | async-start | bytes 6291456 | tf_op jit(solution)/shard_map/all_to_all | solution.py:112
  175.2 0.9 copy-start.2
  261.4 5.7 %copy-start.5 = (f32[1536,4]{0,1:T(4,128)S(1)}, f32[1536,4]{0,1:T(4,128)}, u32[]{:S(2)}) copy-start(f32[1536,4]{0,1:T(4,128)} %param.21) | copy-start | bytes 73732
  261.4 75.7 %all-to-all-start.3 = ((bf16[16,64,1536]{2,1,0:T(8,128)(2,1)}), bf16[16,64,1536]{2,1,0:T(8,128)(2,1)}, u32[]{:S(2)}, u32[]{:S(2)}) async-start(bf16[16,64,1536]{2,1,0:T(8,128)(2,1)} %bitcast.116), calls=%async_computation.3 | async-start | bytes 6291456 | tf_op jit(solution)/shard_map/all_to_all | solution.py:124
  339.6 5.8 %copy-start.3 = (f32[128,1536]{1,0:T(8,128)S(1)}, f32[128,1536]{1,0:T(8,128)}, u32[]{:S(2)}) copy-start(f32[128,1536]{1,0:T(8,128)} %copy-done.2) | copy-start | bytes 2359300
